TPU v7x, 32 devices: a whole 2x2x4 slice. The times are simulated.
32 devices in a mesh: tok: 8 (over y, x, core), head: 4 (over z).
Axes of the slice: x: 2, y: 2, z: 4, core: 2. Of those that a mesh axis runs over, the one named last changes fastest.
Arguments:
- pre_tokens: bfloat16 [8192, 2048], P('tok'), may hold values from -6 to 6
- dec_tokens: bfloat16 [16, 2048], P('tok'), may hold values from -6 to 6
- attn_gain: float32 [2048], replicated, may hold values from 0.1 to 1.9
- mlp_gain: float32 [2048], replicated, may hold values from 0.1 to 1.9
- w_qkv: bfloat16 [3, 2048, 2048], P(None, 'head', 'tok'), may hold values from -0.125 to 0.125
- w_out: bfloat16 [2048, 2048], P('tok', 'head'), may hold values from -0.125 to 0.125
- w_gate_up: bfloat16 [2, 8192, 2048], P(None, 'head', 'tok'), may hold values from -0.125 to 0.125
- w_down: bfloat16 [2048, 8192], P('tok', 'head'), may hold values from -0.0625 to 0.0625
- pre_cache: bfloat16 [8, 2, 2048, 2048], P('tok', None, None, 'head'), may hold values from -60 to 60
- dec_cache: bfloat16 [16, 2, 4096, 2048], P('tok', None, None, 'head'), may hold values from -60 to 60
- pre_order: int32 [8], replicated, may hold values from 0 to 7, each once
- dec_order: int32 [16], replicated, may hold values from 0 to 15, each once
- pre_offsets: int32 [8], P('tok'), may hold values from 2 to 2048, as said below
- dec_lengths: int32 [16], P('tok'), may hold values from 2 to 4096, as said below
Outputs:
- pre_out: bfloat16 [8192, 2048], P('tok')
- dec_out: bfloat16 [16, 2048], P('tok')
Inputs may be any that keep to these rules, and one draw needn't show every extreme that they name: `pre_order`: the prefill request at position k is handled with the caches of position k, which lie on index k of tok. `dec_order`: positions k of one index of tok are those with k // 2 equal to it. `pre_offsets`: some position reaches 2048. `dec_lengths`: some position reaches 4096.
All inputs are finite; a program needn't handle non-finite values.
Results may differ from a plain program's by a relative error of at most 0.013.
Values may be sent and summed in bfloat16 or wider, within the bound.
A program may use at most 192 MiB of HBM per device.

v0:
```python
import jax
import jax.numpy as jnp
from jax import lax
from jax.sharding import PartitionSpec as P

HD = 64
BLOCK = 512
rope_base = 130000.0
norm_eps = 1e-05
masked_score = -1e30


def rotate(values, positions):
    width = values.shape[-1]
    half = width // 2
    freqs = rope_base ** (-(jnp.arange(half, dtype=jnp.float32) * 2.0 / width))
    angles = positions.astype(jnp.float32)[:, None] * freqs[None, :]
    cosine = jnp.cos(angles)[:, None, :]
    sine = jnp.sin(angles)[:, None, :]
    first = values[..., :half]
    second = values[..., half:]
    return jnp.concatenate(
        [first * cosine - second * sine, second * cosine + first * sine], axis=-1
    )


def rms_norm(rows, gain):
    rows = rows.astype(jnp.float32)
    factor = lax.rsqrt(jnp.mean(rows * rows, axis=-1, keepdims=True) + norm_eps)
    return (rows * factor * gain).astype(jnp.bfloat16)


def fold_rows(inputs, weights):
    return jnp.einsum(
        "td,kcd->ktc",
        inputs,
        lax.all_gather(weights, "tok", axis=2, tiled=True),
        preferred_element_type=jnp.float32,
    )


def map_rows(inputs, weights):
    return jnp.einsum(
        "tc,dc->td",
        inputs,
        lax.all_gather(weights, "tok", axis=0, tiled=True),
        preferred_element_type=jnp.float32,
    )


def over_heads(partial_value):
    return lax.psum(partial_value.astype(jnp.bfloat16), "head").astype(jnp.float32)


def attend_local(query, keys_new, values_new, positions, self_mask, cache, limit):
    rows_q = query.shape[0]
    heads = query.shape[1] // HD
    scale = 1.0 / jnp.sqrt(jnp.float32(HD))
    q_rot = rotate(query.reshape(rows_q, heads, HD).astype(jnp.float32), positions).astype(
        jnp.bfloat16
    )
    k_rot = rotate(keys_new.reshape(rows_q, heads, HD).astype(jnp.float32), positions).astype(
        jnp.bfloat16
    )
    v_new = values_new.reshape(rows_q, heads, HD)
    scores = jnp.einsum("qhd,khd->hqk", q_rot, k_rot, preferred_element_type=jnp.float32) * scale
    scores = jnp.where(self_mask[None], scores, masked_score)
    top = jnp.max(scores, axis=-1)
    weights = jnp.exp(scores - top[..., None])
    total = jnp.sum(weights, axis=-1)
    mixed = jnp.einsum(
        "hqk,khd->hqd", weights.astype(jnp.bfloat16), v_new, preferred_element_type=jnp.float32
    )
    cached = cache.reshape(2, cache.shape[1], heads, HD)

    def one_block(index, state):
        top_now, total_now, mixed_now = state
        begin = index * BLOCK
        keys_block = lax.dynamic_slice_in_dim(cached[0], begin, BLOCK, 0)
        values_block = lax.dynamic_slice_in_dim(cached[1], begin, BLOCK, 0)
        block_scores = (
            jnp.einsum("qhd,khd->hqk", q_rot, keys_block, preferred_element_type=jnp.float32)
            * scale
        )
        live = begin + jnp.arange(BLOCK, dtype=jnp.int32) < limit
        block_scores = jnp.where(live[None, None, :], block_scores, masked_score)
        new_top = jnp.maximum(top_now, jnp.max(block_scores, axis=-1))
        factor = jnp.exp(top_now - new_top)
        block_weights = jnp.exp(block_scores - new_top[..., None])
        total_next = total_now * factor + jnp.sum(block_weights, axis=-1)
        mixed_next = mixed_now * factor[..., None] + jnp.einsum(
            "hqk,khd->hqd",
            block_weights.astype(jnp.bfloat16),
            values_block,
            preferred_element_type=jnp.float32,
        )
        return (new_top, total_next, mixed_next)

    block_count = cache.shape[1] // BLOCK
    top, total, mixed = lax.fori_loop(0, block_count, one_block, (top, total, mixed))
    result = mixed / total[..., None]
    return jnp.transpose(result, (1, 0, 2)).reshape(rows_q, heads * HD).astype(jnp.bfloat16)


def on_device(
    pre_tokens,
    dec_tokens,
    attn_gain,
    mlp_gain,
    w_qkv,
    w_out,
    w_gate_up,
    w_down,
    pre_cache,
    dec_cache,
    pre_order,
    dec_order,
    pre_offsets,
    dec_lengths,
):
    tok_count = lax.axis_size("tok")
    tok_index = lax.axis_index("tok")
    span_rows = pre_tokens.shape[0]
    piece_len = span_rows // tok_count
    dec_local = dec_tokens.shape[0]
    dec_total = dec_order.shape[0]
    group_width = w_qkv.shape[1]
    rows = jnp.concatenate([pre_tokens, dec_tokens], axis=0)
    normed = rms_norm(rows, attn_gain)
    projected = fold_rows(normed, w_qkv).astype(jnp.bfloat16)
    pre_part = projected[:, :span_rows].reshape(3, tok_count, piece_len, group_width)
    pre_send = jnp.take(pre_part, pre_order, axis=1)
    dec_part = projected[:, span_rows:]
    dec_send = jnp.broadcast_to(dec_part[:, None], (3, tok_count, dec_local, group_width))
    pre_recv, dec_recv = (
        lax.all_to_all(pre_send, "tok", split_axis=1, concat_axis=1, tiled=True),
        lax.all_to_all(dec_send, "tok", split_axis=1, concat_axis=1, tiled=True),
    )
    pre_recv = pre_recv.reshape(3, span_rows, group_width)
    dec_recv = dec_recv.reshape(3, dec_total, group_width)
    offset_now = pre_offsets[0]
    pre_positions = offset_now + jnp.arange(span_rows, dtype=jnp.int32)
    causal = (
        jnp.arange(span_rows, dtype=jnp.int32)[None, :]
        <= jnp.arange(span_rows, dtype=jnp.int32)[:, None]
    )
    pre_att = attend_local(
        pre_recv[0], pre_recv[1], pre_recv[2], pre_positions, causal, pre_cache[0], offset_now
    )
    own_slots = lax.dynamic_slice_in_dim(dec_order, tok_index * dec_local, dec_local)
    dec_mine = jnp.take(dec_recv, own_slots, axis=1)
    self_only = jnp.ones((1, 1), jnp.bool_)
    dec_results = []
    for request in range(dec_local):
        length_now = dec_lengths[request]
        dec_results.append(
            attend_local(
                dec_mine[0, request : request + 1],
                dec_mine[1, request : request + 1],
                dec_mine[2, request : request + 1],
                dec_lengths[request : request + 1],
                self_only,
                dec_cache[request],
                length_now,
            )
        )
    dec_att = jnp.concatenate(dec_results, axis=0)
    picker = (jnp.arange(dec_total, dtype=jnp.int32)[:, None] == own_slots[None, :]).astype(
        jnp.bfloat16
    )
    dec_back = (
        jnp.dot(picker, dec_att, preferred_element_type=jnp.float32)
        .astype(jnp.bfloat16)
        .reshape(tok_count, dec_local, group_width)
    )
    pre_back = pre_att.reshape(tok_count, piece_len, group_width)
    pre_ret, dec_ret = (
        lax.all_to_all(pre_back, "tok", split_axis=0, concat_axis=0, tiled=True),
        lax.all_to_all(dec_back, "tok", split_axis=0, concat_axis=0, tiled=True),
    )
    slot_range = jnp.arange(tok_count, dtype=jnp.int32)
    inverse = jnp.sum(
        jnp.where(pre_order[None, :] == slot_range[:, None], slot_range[None, :], 0), axis=1
    )
    pre_mixed = jnp.take(pre_ret, inverse, axis=0).reshape(span_rows, group_width)
    dec_mixed = jnp.sum(dec_ret.astype(jnp.float32), axis=0).astype(jnp.bfloat16)
    attended = jnp.concatenate([pre_mixed, dec_mixed], axis=0)
    resid = rows.astype(jnp.float32) + over_heads(map_rows(attended, w_out))
    mlp_in = rms_norm(resid, mlp_gain)
    gate_up = fold_rows(mlp_in, w_gate_up)
    hidden = (jax.nn.silu(gate_up[0]) * gate_up[1]).astype(jnp.bfloat16)
    final = (resid + over_heads(map_rows(hidden, w_down))).astype(jnp.bfloat16)
    return (final[:span_rows], final[span_rows:])


def solution(mesh):
    placed = (
        P("tok", None),
        P("tok", None),
        P(),
        P(),
        P(None, "head", "tok"),
        P("tok", "head"),
        P(None, "head", "tok"),
        P("tok", "head"),
        P("tok", None, None, "head"),
        P("tok", None, None, "head"),
        P(),
        P(),
        P("tok"),
        P("tok"),
    )
    return jax.shard_map(
        on_device,
        mesh=mesh,
        in_specs=placed,
        out_specs=(P("tok", None), P("tok", None)),
        check_vma=False,
    )
```

profile of v0, /device:TPU:0, one launch (start us, length us, event | category | flops | bytes accessed | tf_op | source)
XLA Modules:
  0.0 917.4 jit_solution(6938060684797594388)
XLA Ops:
  15.1 6.3 copy.63
  22.7 11.3 %fusion.97 = (bf16[1,2,4096,512]{3,2,1,0:T(8,128)(2,1)}, bf16[1,2,4096,512]{3,2,1,0:T(8,128)(2,1)}) fusion(bf16[2,2,4096,512]{3,2,1,0:T(8,128)(2,1)} %param.29), kind=kLoop, calls=%fused_computation.196 | loop fusion | bytes 33554432 | tf_op jit(solution)/shard_map/slice | solution.py:163
  34.1 11.3 %copy.94 = bf16[1,2,4096,512]{2,3,1,0:T(8,128)(2,1)} copy(bf16[1,2,4096,512]{3,2,1,0:T(8,128)(2,1)} %get-tuple-element.511) | data formatting | bytes 16777216
  45.4 18.9 %copy.67 = bf16[2,4096,8,64]{3,2,1,0:T(8,128)(2,1)} copy(bf16[2,4096,8,64]{1,3,2,0:T(8,128)(2,1)} %bitcast.220) | data formatting | bytes 16777216 | tf_op jit(solution)/shard_map/while | solution.py:100
  64.9 11.7 %copy.95 = bf16[1,2,4096,512]{2,3,1,0:T(8,128)(2,1)} copy(bf16[1,2,4096,512]{3,2,1,0:T(8,128)(2,1)} %get-tuple-element.512) | data formatting | bytes 16777216
  76.6 19.0 %copy.69 = bf16[2,4096,8,64]{3,2,1,0:T(8,128)(2,1)} copy(bf16[2,4096,8,64]{1,3,2,0:T(8,128)(2,1)} %bitcast.221) | data formatting | bytes 16777216 | tf_op jit(solution)/shard_map/while | solution.py:100
  96.2 10.4 %fusion.59 = bf16[3,1026,512]{2,1,0:T(8,128)(2,1)S(1)} fusion(bf16[3,512,2048]{2,1,0:T(8,128)(2,1)} %all-gather.5.cloned.1.call-done, f32[2048]{0:T(1024)S(1)} %copy-done.10, f32[1026]{0:T(1024)S(1)} %add_rsqrt_fusion.1, bf16[2,2048]{1,0:T(2,128)(2,1)S(1)} %copy-done.4, bf16[1024,2048]{1,0:T(8,128)(2,1)} %param.20), kind=kOutput, calls=%fused_computation.96 | convolution fusion | flops 6471318528 | bytes 13658120 | tf_op jit(solution)/shard_map/td,kcd->ktc/dot_general | solution.py:34
  107.5 5.7 all-to-all-start.2
  115.5 3.9 select_bitcast_fusion
  119.4 4.2 all-to-all-start
  125.0 66.9 %while.52 = (s32[]{:T(128)}, f32[8,1]{0,1:T(1,128)S(1)}, f32[8,1]{0,1:T(1,128)S(1)}, f32[8,1,64]{2,1,0:T(1,128)S(1)}, s32[]{:T(128)}, /*index=5*/bf16[2,4096,8,6...) while((s32[]{:T(128)}, f32[8,1]{0,1:T(1,128)S(1)}, ...), condition=%wide.region_11.12_spmd, body=%wide.region_8.11_spmd.sunk | while | flops 1083422 | bytes 19995780 | solution.py:100
  125.0 6.5 fusion.138
  133.3 6.5 fusion.138
  141.7 6.5 fusion.138
  150.1 6.5 fusion.138
  158.4 6.5 fusion.138
  166.8 6.5 fusion.138
  175.2 6.5 fusion.138
  183.5 6.5 fusion.138
  192.5 66.4 %while.53 = (s32[]{:T(128)}, f32[8,1]{0,1:T(1,128)S(1)}, f32[8,1]{0,1:T(1,128)S(1)}, f32[8,1,64]{2,1,0:T(1,128)S(1)}, s32[]{:T(128)}, /*index=5*/bf16[2,4096,8,6...) while((s32[]{:T(128)}, f32[8,1]{0,1:T(1,128)S(1)}, ...), condition=%wide.region_15.16_spmd, body=%wide.region_12.15_spmd.sunk | while | flops 1083422 | bytes 19995780 | solution.py:100
  192.5 6.5 fusion.147
  200.8 6.5 fusion.147
  209.1 6.5 fusion.147
  217.4 6.5 fusion.147
  225.7 6.5 fusion.147
  234.0 6.5 fusion.147
  242.3 6.5 fusion.147
  250.6 6.5 fusion.147
  260.0 4.7 all-to-all-start.3
  284.8 13.6 %fusion.39 = (f32[8,1024]{1,0:T(8,128)S(1)}, f32[8,1024,1024]{1,2,0:T(8,128)}) fusion(pred[1024,1024]{0,1:T(8,128)(4,1)S(1)} %copy-done, bf16[1024,8,32]{0,2,1:T(8,128)(2,1)S(1)} %get-tuple-element.520, bf16[1024,8,32]{0,2,1:T(8,128)(2,1)S(1)} %get-tuple-element.521, bf16[1024,8,32]{0,2,1:T(8,128)(2,1)S(1)} %get-tuple-element.517, ...), kind=kOutput, calls=%fused_computation.66 | convolution fusion | flops 1103093760 | bytes 36732928 | tf_op jit(solution)/shard_map/qhd,khd->hqk/dot_general | solution.py:66
  298.4 14.3 %fusion.41 = f32[8,1024]{1,0:T(8,128)S(1)} fusion(f32[8,1024,1024]{1,2,0:T(8,128)} %get-tuple-element.545, f32[8,1024]{1,0:T(8,128)S(1)} %get-tuple-element.790, pred[1024,1024]{0,1:T(8,128)(4,1)S(1)} %copy-done), kind=kLoop, calls=%fused_computation.68 | loop fusion | flops 33546240 | bytes 34668544 | tf_op jit(solution)/shard_map/reduce_sum | solution.py:70
  312.7 16.0 %fusion.42 = f32[8,1024,64]{1,2,0:T(8,128)} fusion(bf16[1024,8,64]{0,2,1:T(8,128)(2,1)S(1)} %copy-done.3, f32[8,1024,1024]{1,2,0:T(8,128)} %get-tuple-element.545, f32[8,1024]{1,0:T(8,128)S(1)} %get-tuple-element.790, pred[1024,1024]{0,1:T(8,128)(4,1)S(1)} %copy-done), kind=kOutput, calls=%fused_computation.69 | convolution fusion | flops 1107296256 | bytes 37781504 | tf_op jit(solution)/shard_map/hqk,khd->hqd/dot_general | solution.py:71
  328.8 63.3 %while.51 = (s32[]{:T(128)}, f32[8,1024]{1,0:T(8,128)S(1)}, f32[8,1024]{1,0:T(8,128)S(1)}, f32[8,1024,64]{1,2,0:T(8,128)}, s32[]{:T(128)}, /*index=5*/bf16[2,204...) while((s32[]{:T(128)}, f32[8,1024]{1,0:T(8,128)S(1)}, ...), condition=%wide.region_7.8_spmd, body=%wide.region_4.7_spmd.sunk | while | flops 1120945152 | bytes 82315496 | solution.py:100
  339.5 3.9 multiply_add_fusion.5
  355.3 3.9 multiply_add_fusion.5
  371.1 3.9 multiply_add_fusion.5
  386.9 3.9 multiply_add_fusion.5
  395.7 4.2 all-to-all-start.1
  400.9 14.4 %all-to-all-done.1 = bf16[8,128,512]{2,1,0:T(8,128)(2,1)S(1)} async-done(((bf16[8,128,512]{2,1,0:T(8,128)(2,1)}), bf16[8,128,512]{2,1,0:T(8,128)(2,1)S(1)}, u32[]{:S(2)}, u32[]{:S(2)}) %all-to-all-start.1) | async-done | bytes 1048608 | tf_op jit(solution)/shard_map/all_to_all | solution.py:178
  416.2 5.9 convolution_convert_fusion.1
  423.4 153.9 %all-reduce.3.cloned.1.call-done = bf16[1026,2048]{1,0:T(8,128)(2,1)} async-done(((bf16[1026,2048]{1,0:T(8,128)(2,1)}), bf16[1026,2048]{1,0:T(8,128)(2,1)}) %all-reduce.3.cloned.1.call-update) | async-done | bytes 4202512 | tf_op jit(solution)/shard_map/psum | solution.py:52
  577.3 4.4 multiply_reduce_fusion
  581.7 89.4 %all-gather.9.cloned.1.call-done = bf16[2,2048,2048]{2,1,0:T(8,128)(2,1)} async-done(((bf16[2,2048,256]{2,1,0:T(8,128)(2,1)}), bf16[2,2048,2048]{2,1,0:T(8,128)(2,1)}) %all-gather.9.cloned.1.call-update) | async-done | bytes 16777232 | tf_op jit(solution)/shard_map/all_gather | solution.py:37
  671.2 25.3 %convolution_bitcast_fusion = f32[2,1026,2048]{2,1,0:T(8,128)} fusion(bf16[2,2048,2048]{2,1,0:T(8,128)(2,1)} %all-gather.9.cloned.1.call-done, bf16[1026,2048]{1,0:T(8,128)(2,1)} %all-reduce.3.cloned.1.call-done, f32[2048]{0:T(1024)S(1)} %copy-done.11, f32[1026]{0:T(1024)S(1)} %add_rsqrt_fusion, bf16[2,2048]{1,0:T(2,128)(2,1)S(1)} %copy-done.5, ...), kind=kOutput, calls=%fused_computation.71 | convolution fusion | flops 17232334848 | bytes 42004488 | tf_op jit(solution)/shard_map/td,kcd->ktc/dot_general | solution.py:34
  696.5 30.8 %all-gather.11.cloned.1.call-done = bf16[2048,2048]{1,0:T(8,128)(2,1)} async-done(((bf16[256,2048]{1,0:T(8,128)(2,1)}), bf16[2048,2048]{1,0:T(8,128)(2,1)}) %all-gather.11.cloned.1.call-update) | async-done | bytes 8388624 | tf_op jit(solution)/shard_map/all_gather | solution.py:46
  727.3 17.7 %convolution_convert_fusion = bf16[1026,2048]{1,0:T(8,128)(2,1)} fusion(bf16[2048,2048]{1,0:T(8,128)(2,1)} %all-gather.11.cloned.1.call-done, f32[2,1026,2048]{2,1,0:T(8,128)} %convolution_bitcast_fusion), kind=kOutput, calls=%fused_computation.85 | convolution fusion | flops 8621420544 | bytes 29401088 | tf_op jit(solution)/shard_map/tc,dc->td/dot_general | solution.py:43
  745.0 156.2 %all-reduce.5.cloned.1.call-done = bf16[1026,2048]{1,0:T(8,128)(2,1)} async-done(((bf16[1026,2048]{1,0:T(8,128)(2,1)}), bf16[1026,2048]{1,0:T(8,128)(2,1)}) %all-reduce.5.cloned.1.call-update) | async-done | bytes 4202512 | tf_op jit(solution)/shard_map/psum | solution.py:52
  901.3 6.2 add_convert_fusion
  (295 shorter events, 120.3 us)
Async XLA Ops:
  7.2 14.2 %copy-start.9 = (s32[16]{0:T(128)S(1)}, s32[16]{0:T(128)}, u32[]{:S(2)}) copy-start(s32[16]{0:T(128)} %param.31) | copy-start | bytes 196
  7.2 14.3 %copy-start.6 = (s32[2]{0:T(128)S(1)}, s32[2]{0:T(128)}, u32[]{:S(2)}) copy-start(s32[2]{0:T(128)} %param.33) | copy-start | bytes 28
  7.2 89.0 %all-gather.5.cloned.1.call-start = ((), (), s32[]{:S(2)}) async-start(), calls=%async_computation.4 | async-start | bytes 7077888 | tf_op jit(solution)/shard_map/all_gather | solution.py:37
  7.9 408.3 %all-gather.7.cloned.1.call-start = ((), (), s32[]{:S(2)}) async-start(), calls=%async_computation.5 | async-start | bytes 2359296 | tf_op jit(solution)/shard_map/all_gather | solution.py:46
  21.5 12.6 %copy-start.7 = (s32[2]{0:T(128)}, s32[2]{0:T(128)S(1)}, u32[]{:S(2)}) copy-start(s32[2]{0:T(128)S(1)} %get-tuple-element.494) | copy-start | bytes 28
  76.6 19.5 %copy-start.4 = (bf16[2,2048]{1,0:T(2,128)(2,1)S(1)}, bf16[2,2048]{1,0:T(2,128)(2,1)}, u32[]{:S(2)}) copy-start(bf16[2,2048]{1,0:T(2,128)(2,1)} %param.21) | copy-start | bytes 24580
  76.6 19.6 %copy-start.10 = (f32[2048]{0:T(1024)S(1)}, f32[2048]{0:T(1024)}, u32[]{:S(2)}) copy-start(f32[2048]{0:T(1024)} %param.22) | copy-start | bytes 24580
  107.5 11.9 %all-to-all-start.2 = ((bf16[3,8,2,512]{3,2,0,1:T(2,128)(2,1)}), bf16[3,8,2,512]{3,2,0,1:T(2,128)(2,1)S(1)}, u32[]{:S(2)}, u32[]{:S(2)}) async-start(bf16[3,8,2,512]{3,2,0,1:T(2,128)(2,1)} %broadcast_in_dim.223), calls=%async_computation.2 | async-start | bytes 98304 | tf_op jit(solution)/shard_map/all_to_all | solution.py:137
  119.4 140.7 %all-to-all-start = ((bf16[3,8,128,512]{3,2,0,1:T(8,128)(2,1)}), bf16[3,8,128,512]{3,2,0,1:T(8,128)(2,1)S(1)}, u32[]{:S(2)}, u32[]{:S(2)}) async-start(bf16[3,8,128,512]{3,2,0,1:T(8,128)(2,1)} %select_bitcast_fusion), calls=%async_computation | async-start | bytes 6291456 | tf_op jit(solution)/shard_map/all_to_all | solution.py:136
  192.5 66.8 %copy-start.8 = (s32[2]{0:T(128)S(1)}, s32[2]{0:T(128)}, u32[]{:S(2)}) copy-start(s32[2]{0:T(128)} %copy-done.7) | copy-start | bytes 28
  260.0 135.7 %all-to-all-start.3 = ((bf16[8,2,512]{2,1,0:T(2,128)(2,1)}), bf16[8,2,512]{2,1,0:T(2,128)(2,1)}, u32[]{:S(2)}, u32[]{:S(2)}) async-start(bf16[8,2,512]{2,1,0:T(2,128)(2,1)} %reshape.531), calls=%async_computation.3 | async-start | bytes 32768 | tf_op jit(solution)/shard_map/all_to_all | solution.py:179
  275.0 9.9 %copy-start = (pred[1024,1024]{0,1:T(8,128)(4,1)S(1)}, pred[1024,1024]{0,1:T(8,128)(4,1)}, u32[]{:S(2)}) copy-start(pred[1024,1024]{0,1:T(8,128)(4,1)} %iota_compare_fusion) | copy-start | bytes 3145732
  298.4 14.3 %copy-start.3 = (bf16[1024,8,64]{0,2,1:T(8,128)(2,1)S(1)}, bf16[1024,8,64]{0,2,1:T(8,128)(2,1)}, u32[]{:S(2)}) copy-start(bf16[1024,8,64]{0,2,1:T(8,128)(2,1)} %reshape_squeeze.8) | copy-start | bytes 3145732
  335.6 3.9 copy-start.1
  343.4 1.3 copy-start.2
  351.4 3.9 copy-start.1
  359.2 1.3 copy-start.2
  367.1 3.9 copy-start.1
  375.0 1.3 copy-start.2
  382.9 3.9 copy-start.1
  390.8 1.3 copy-start.2
  392.1 7.9 copy-start.12
  395.7 19.6 %all-to-all-start.1 = ((bf16[8,128,512]{2,1,0:T(8,128)(2,1)}), bf16[8,128,512]{2,1,0:T(8,128)(2,1)S(1)}, u32[]{:S(2)}, u32[]{:S(2)}) async-start(bf16[8,128,512]{2,1,0:T(8,128)(2,1)} %copy.64), calls=%async_computation.1 | async-start | bytes 2097152 | tf_op jit(solution)/shard_map/all_to_all | solution.py:178
  399.9 177.3 %all-reduce.3.cloned.1.call-start = ((), (), s32[]{:S(2)}) async-start(), calls=%async_computation.6 | async-start | bytes 8454144 | tf_op jit(solution)/shard_map/psum | solution.py:52
  416.2 161.1 %copy-start.5 = (bf16[2,2048]{1,0:T(2,128)(2,1)S(1)}, bf16[2,2048]{1,0:T(2,128)(2,1)}, u32[]{:S(2)}) copy-start(bf16[2,2048]{1,0:T(2,128)(2,1)} %param.21) | copy-start | bytes 24580
  422.2 249.0 %copy-start.11 = (f32[2048]{0:T(1024)S(1)}, f32[2048]{0:T(1024)}, u32[]{:S(2)}) copy-start(f32[2048]{0:T(1024)} %param.23) | copy-start | bytes 24580
  422.2 249.0 %all-gather.9.cloned.1.call-start = ((), (), s32[]{:S(2)}) async-start(), calls=%async_computation.7 | async-start | bytes 18874368 | tf_op jit(solution)/shard_map/all_gather | solution.py:37
  422.8 304.6 %all-gather.11.cloned.1.call-start = ((), (), s32[]{:S(2)}) async-start(), calls=%async_computation.8 | async-start | bytes 9437184 | tf_op jit(solution)/shard_map/all_gather | solution.py:46
  423.4 477.9 %all-reduce.5.cloned.1.call-start = ((), (), s32[]{:S(2)}) async-start(), calls=%async_computation.9 | async-start | bytes 8454144 | tf_op jit(solution)/shard_map/psum | solution.py:52
Sparse Core Ops, SparseCore 0:
  9.9 49.3 all-gather.4
  61.2 27.9 all-gather.6
  422.3 154.9 all-reduce.2
  579.0 92.1 all-gather.8
  672.9 54.3 all-gather.10
  745.2 156.0 all-reduce.4
where the time goes:
time: 928 us; the launch traced here: 917 us
  waiting for transfers between devices  447 us (48%)
  local copies, waits for them, and re-layouts  227 us (24%)
  matrix products  129 us (14%)
  other arithmetic  77.7 us (8%)
  starting transfers between devices  19 us (2%)
  between operations  16.5 us (2%)
    psum x2, waiting for transfers between devices, over_heads(): lax.psum(partial_value.astype(jnp.bfloat16), 'head').astype(jnp.float32)  310 us
    slice x20, local copies, waits for them, and re-layouts, one_block(): values_block = lax.dynamic_slice_in_dim(cached[1], begin, BLOCK, 0)  115 us
    all_gather x2, waiting for transfers between devices, fold_rows(): lax.all_gather(weights, 'tok', axis=2, tiled=True)  89.5 us
    while x2, local copies, waits for them, and re-layouts, attend_local(): lax.fori_loop(0, block_count, one_block, (top, total, mixed))  37.9 us
    dot_general x2, matrix products, fold_rows(): jnp.einsum('td,kcd->ktc', inputs, lax.all_gather(weights, 'tok', axis=2,...  35.7 us
    all_gather x2, waiting for transfers between devices, map_rows(): lax.all_gather(weights, 'tok', axis=0, tiled=True)  30.8 us
    unnamed x26, local copies, waits for them, and re-layouts  29.5 us
    dot_general x2, matrix products, map_rows(): jnp.einsum('tc,dc->td', inputs, lax.all_gather(weights, 'tok', axis=0, ti...  23.6 us
  transfers between devices with their start and end apart: 10, of which 5 were waited for; matrix products, arithmetic and copies ran while one was open for 43% of the time, Pallas kernels for 0%

commit v1 on v0

--- a/solution.py
+++ b/solution.py
@@ -49,7 +49,9 @@
 
 
 def over_heads(partial_value):
-    return lax.psum(partial_value.astype(jnp.bfloat16), "head").astype(jnp.float32)
+    return jnp.sum(lax.all_gather(partial_value.astype(jnp.bfloat16), "head"), axis=0).astype(
+        jnp.float32
+    )
 
 
 def attend_local(query, keys_new, values_new, positions, self_mask, cache, limit):

time: 928 us -> 1210 us (1.30)
  waiting for transfers between devices: 447 us -> 703 us
  other arithmetic: 77.7 us -> 103 us
    all_gather x0 -> x2, waiting for transfers between devices: none -> 579 us  [over_heads(): lax.all_gather(partial_value.astype(jnp.bfloat16), 'head')]
    psum x2 -> x0, waiting for transfers between devices: 310 us -> none  [over_heads(): lax.psum(partial_value.astype(jnp.bfloat16), 'head').astype(jnp.float32)]
    reduce_sum x0 -> x2, other arithmetic: none -> 24.6 us  [over_heads(): jnp.sum(lax.all_gather(partial_value.astype(jnp.bfloat16), 'head'), axis=0)]
    all_gather x2, waiting for transfers between devices: 89.5 us -> 76.8 us  [fold_rows(): lax.all_gather(weights, 'tok', axis=2, tiled=True)]
  transfers between devices with their start and end apart: 10 -> 10, of which waited for: 5 -> 5; matrix products, arithmetic and copies ran while one was open for 43% -> 34% of each run, Pallas kernels for 0% -> 0%
where the time goes in v1:
time: 1210 us; the launch traced here: 1200 us
  waiting for transfers between devices  703 us (58%)
  local copies, waits for them, and re-layouts  227 us (19%)
  matrix products  129 us (11%)
  other arithmetic  103 us (9%)
  starting transfers between devices  19.2 us (2%)
  between operations  16.5 us (1%)
    all_gather x2, waiting for transfers between devices, over_heads(): lax.all_gather(partial_value.astype(jnp.bfloat16), 'head')  579 us
    slice x20, local copies, waits for them, and re-layouts, one_block(): values_block = lax.dynamic_slice_in_dim(cached[1], begin, BLOCK, 0)  115 us
    all_gather x2, waiting for transfers between devices, fold_rows(): lax.all_gather(weights, 'tok', axis=2, tiled=True)  76.8 us
    while x2, local copies, waits for them, and re-layouts, attend_local(): lax.fori_loop(0, block_count, one_block, (top, total, mixed))  37.9 us
    dot_general x2, matrix products, fold_rows(): jnp.einsum('td,kcd->ktc', inputs, lax.all_gather(weights, 'tok', axis=2,...  35.7 us
    all_gather x2, waiting for transfers between devices, map_rows(): lax.all_gather(weights, 'tok', axis=0, tiled=True)  30.9 us
    unnamed x26, local copies, waits for them, and re-layouts  29.5 us
    reduce_sum x2, other arithmetic, over_heads(): jnp.sum(lax.all_gather(partial_value.astype(jnp.bfloat16), 'head'), axis=0)  24.6 us
  transfers between devices with their start and end apart: 10, of which 5 were waited for; matrix products, arithmetic and copies ran while one was open for 34% of the time, Pallas kernels for 0%

profile of v1, /device:TPU:0, one launch (start us, length us, event | category | flops | bytes accessed | tf_op | source)
XLA Modules:
  0.0 1198.5 jit_solution(6277692567860076559)
XLA Ops:
  15.1 6.3 copy.63
  22.7 11.3 fusion.99
  34.1 11.3 copy.94
  45.4 18.9 %copy.67 = bf16[2,4096,8,64]{3,2,1,0:T(8,128)(2,1)} copy(bf16[2,4096,8,64]{1,3,2,0:T(8,128)(2,1)} %bitcast.224) | data formatting | bytes 16777216 | tf_op jit(solution)/shard_map/while | solution.py:102
  64.9 11.7 copy.95
  76.6 19.0 %copy.69 = bf16[2,4096,8,64]{3,2,1,0:T(8,128)(2,1)} copy(bf16[2,4096,8,64]{1,3,2,0:T(8,128)(2,1)} %bitcast.225) | data formatting | bytes 16777216 | tf_op jit(solution)/shard_map/while | solution.py:102
  96.2 10.4 fusion.61
  107.5 5.7 all-to-all-start.2
  119.4 4.2 all-to-all-start
  125.0 66.9 %while.52 = (s32[]{:T(128)}, f32[8,1]{0,1:T(1,128)S(1)}, f32[8,1]{0,1:T(1,128)S(1)}, f32[8,1,64]{2,1,0:T(1,128)S(1)}, s32[]{:T(128)}, /*index=5*/bf16[2,4096,8,6...) while((s32[]{:T(128)}, f32[8,1]{0,1:T(1,128)S(1)}, ...), condition=%wide.region_11.12_spmd, body=%wide.region_8.11_spmd.sunk | while | flops 1083422 | bytes 19995780 | solution.py:102
  125.0 6.5 fusion.140
  133.3 6.5 fusion.140
  141.7 6.5 fusion.140
  150.1 6.5 fusion.140
  158.4 6.5 fusion.140
  166.8 6.5 fusion.140
  175.2 6.5 fusion.140
  183.5 6.5 fusion.140
  192.5 66.4 %while.53 = (s32[]{:T(128)}, f32[8,1]{0,1:T(1,128)S(1)}, f32[8,1]{0,1:T(1,128)S(1)}, f32[8,1,64]{2,1,0:T(1,128)S(1)}, s32[]{:T(128)}, /*index=5*/bf16[2,4096,8,6...) while((s32[]{:T(128)}, f32[8,1]{0,1:T(1,128)S(1)}, ...), condition=%wide.region_15.16_spmd, body=%wide.region_12.15_spmd.sunk | while | flops 1083422 | bytes 19995780 | solution.py:102
  192.5 6.5 fusion.149
  200.8 6.5 fusion.149
  209.1 6.5 fusion.149
  217.4 6.5 fusion.149
  225.7 6.5 fusion.149
  234.0 6.5 fusion.149
  242.3 6.5 fusion.149
  250.6 6.5 fusion.149
  260.0 4.7 all-to-all-start.3
  284.8 13.6 %fusion.39 = (f32[8,1024]{1,0:T(8,128)S(1)}, f32[8,1024,1024]{1,2,0:T(8,128)}) fusion(pred[1024,1024]{0,1:T(8,128)(4,1)S(1)} %copy-done, bf16[1024,8,32]{0,2,1:T(8,128)(2,1)S(1)} %get-tuple-element.520, bf16[1024,8,32]{0,2,1:T(8,128)(2,1)S(1)} %get-tuple-element.521, bf16[1024,8,32]{0,2,1:T(8,128)(2,1)S(1)} %get-tuple-element.517, ...), kind=kOutput, calls=%fused_computation.66 | convolution fusion | flops 1103093760 | bytes 36732928 | tf_op jit(solution)/shard_map/qhd,khd->hqk/dot_general | solution.py:68
  298.4 14.3 %fusion.41 = f32[8,1024]{1,0:T(8,128)S(1)} fusion(f32[8,1024,1024]{1,2,0:T(8,128)} %get-tuple-element.545, f32[8,1024]{1,0:T(8,128)S(1)} %get-tuple-element.790, pred[1024,1024]{0,1:T(8,128)(4,1)S(1)} %copy-done), kind=kLoop, calls=%fused_computation.68 | loop fusion | flops 33546240 | bytes 34668544 | tf_op jit(solution)/shard_map/reduce_sum | solution.py:72
  312.7 16.0 %fusion.42 = f32[8,1024,64]{1,2,0:T(8,128)} fusion(bf16[1024,8,64]{0,2,1:T(8,128)(2,1)S(1)} %copy-done.3, f32[8,1024,1024]{1,2,0:T(8,128)} %get-tuple-element.545, f32[8,1024]{1,0:T(8,128)S(1)} %get-tuple-element.790, pred[1024,1024]{0,1:T(8,128)(4,1)S(1)} %copy-done), kind=kOutput, calls=%fused_computation.69 | convolution fusion | flops 1107296256 | bytes 37781504 | tf_op jit(solution)/shard_map/hqk,khd->hqd/dot_general | solution.py:73
  328.8 63.3 %while.51 = (s32[]{:T(128)}, f32[8,1024]{1,0:T(8,128)S(1)}, f32[8,1024]{1,0:T(8,128)S(1)}, f32[8,1024,64]{1,2,0:T(8,128)}, s32[]{:T(128)}, /*index=5*/bf16[2,204...) while((s32[]{:T(128)}, f32[8,1024]{1,0:T(8,128)S(1)}, ...), condition=%wide.region_7.8_spmd, body=%wide.region_4.7_spmd.sunk | while | flops 1120945152 | bytes 82315496 | solution.py:102
  355.3 3.9 multiply_add_fusion.5
  371.1 3.9 multiply_add_fusion.5
  386.9 3.9 multiply_add_fusion.5
  395.7 4.2 all-to-all-start.1
  400.9 14.4 %all-to-all-done.1 = bf16[8,128,512]{2,1,0:T(8,128)(2,1)S(1)} async-done(((bf16[8,128,512]{2,1,0:T(8,128)(2,1)}), bf16[8,128,512]{2,1,0:T(8,128)(2,1)S(1)}, u32[]{:S(2)}, u32[]{:S(2)}) %all-to-all-start.1) | async-done | bytes 1048608 | tf_op jit(solution)/shard_map/all_to_all | solution.py:180
  416.2 5.9 fusion.50
  423.6 288.1 %all-gather.19.cloned.1.call-done = bf16[4,1026,2048]{2,1,0:T(8,128)(2,1)} async-done(((bf16[1,1026,2048]{2,1,0:T(8,128)(2,1)}), bf16[4,1026,2048]{2,1,0:T(8,128)(2,1)}) %all-gather.19.cloned.1.call-update) | async-done | bytes 16810000 | tf_op jit(solution)/shard_map/all_gather | solution.py:52
  711.7 12.6 %reduce_sum.132 = bf16[1026,2048]{1,0:T(8,128)(2,1)} reduce(bf16[4,1026,2048]{2,1,0:T(8,128)(2,1)} %all-gather.19.cloned.1.call-done, bf16[]{:T(256)} %constant.259.clone.1), dimensions={0}, to_apply=%region_17.18 | reduce | flops 6303744 | bytes 21012482 | tf_op jit(solution)/shard_map/reduce_sum | solution.py:52
  724.3 4.6 multiply_reduce_fusion
  728.9 76.8 %all-gather.15.cloned.1.call-done = bf16[2,2048,2048]{2,1,0:T(8,128)(2,1)} async-done(((bf16[2,2048,256]{2,1,0:T(8,128)(2,1)}), bf16[2,2048,2048]{2,1,0:T(8,128)(2,1)}) %all-gather.15.cloned.1.call-update) | async-done | bytes 16777232 | tf_op jit(solution)/shard_map/all_gather | solution.py:37
  805.7 25.3 %convolution_bitcast_fusion = f32[2,1026,2048]{2,1,0:T(8,128)} fusion(bf16[2,2048,2048]{2,1,0:T(8,128)(2,1)} %all-gather.15.cloned.1.call-done, bf16[1026,2048]{1,0:T(8,128)(2,1)} %reduce_sum.132, f32[2048]{0:T(1024)S(1)} %copy-done.11, f32[1026]{0:T(1024)S(1)} %add_rsqrt_fusion, bf16[2,2048]{1,0:T(2,128)(2,1)S(1)} %copy-done.5, bf16[1024,2048]{1,0:T(8,128)(2,1)} %param.20), kind=kOutput, calls=%fused_computation.71 | convolution fusion | flops 17232334848 | bytes 42004488 | tf_op jit(solution)/shard_map/td,kcd->ktc/dot_general | solution.py:34
  831.0 30.8 %all-gather.17.cloned.1.call-done = bf16[2048,2048]{1,0:T(8,128)(2,1)} async-done(((bf16[256,2048]{1,0:T(8,128)(2,1)}), bf16[2048,2048]{1,0:T(8,128)(2,1)}) %all-gather.17.cloned.1.call-update) | async-done | bytes 8388624 | tf_op jit(solution)/shard_map/all_gather | solution.py:46
  861.8 17.7 %fusion.51 = bf16[1,1026,2048]{2,1,0:T(8,128)(2,1)} fusion(bf16[2048,2048]{1,0:T(8,128)(2,1)} %all-gather.17.cloned.1.call-done, f32[2,1026,2048]{2,1,0:T(8,128)} %convolution_bitcast_fusion), kind=kOutput, calls=%fused_computation.88 | convolution fusion | flops 8621420544 | bytes 29401088 | tf_op jit(solution)/shard_map/tc,dc->td/dot_general | solution.py:43
  879.6 290.7 %all-gather.21.cloned.1.call-done = bf16[4,1026,2048]{2,1,0:T(8,128)(2,1)} async-done(((bf16[1,1026,2048]{2,1,0:T(8,128)(2,1)}), bf16[4,1026,2048]{2,1,0:T(8,128)(2,1)}) %all-gather.21.cloned.1.call-update) | async-done | bytes 16810000 | tf_op jit(solution)/shard_map/all_gather | solution.py:52
  1170.2 12.1 %reduce_sum.134 = bf16[1026,2048]{1,0:T(8,128)(2,1)} reduce(bf16[4,1026,2048]{2,1,0:T(8,128)(2,1)} %all-gather.21.cloned.1.call-done, bf16[]{:T(256)} %constant.259.clone.1), dimensions={0}, to_apply=%region_19.20 | reduce | flops 6303744 | bytes 21012482 | tf_op jit(solution)/shard_map/reduce_sum | solution.py:52
  1182.3 6.2 add_convert_fusion
  (297 shorter events, 128.3 us)
Async XLA Ops:
  7.2 14.2 %copy-start.9 = (s32[16]{0:T(128)S(1)}, s32[16]{0:T(128)}, u32[]{:S(2)}) copy-start(s32[16]{0:T(128)} %param.31) | copy-start | bytes 196
  7.2 14.3 %copy-start.6 = (s32[2]{0:T(128)S(1)}, s32[2]{0:T(128)}, u32[]{:S(2)}) copy-start(s32[2]{0:T(128)} %param.33) | copy-start | bytes 28
  7.2 89.0 %all-gather.11.cloned.1.call-start = ((), (), s32[]{:S(2)}) async-start(), calls=%async_computation.4 | async-start | bytes 7077888 | tf_op jit(solution)/shard_map/all_gather | solution.py:37
  7.9 408.3 %all-gather.13.cloned.1.call-start = ((), (), s32[]{:S(2)}) async-start(), calls=%async_computation.5 | async-start | bytes 2359296 | tf_op jit(solution)/shard_map/all_gather | solution.py:46
  21.5 12.6 %copy-start.7 = (s32[2]{0:T(128)}, s32[2]{0:T(128)S(1)}, u32[]{:S(2)}) copy-start(s32[2]{0:T(128)S(1)} %get-tuple-element.494) | copy-start | bytes 28
  76.6 19.5 %copy-start.4 = (bf16[2,2048]{1,0:T(2,128)(2,1)S(1)}, bf16[2,2048]{1,0:T(2,128)(2,1)}, u32[]{:S(2)}) copy-start(bf16[2,2048]{1,0:T(2,128)(2,1)} %param.21) | copy-start | bytes 24580
  76.6 19.6 %copy-start.10 = (f32[2048]{0:T(1024)S(1)}, f32[2048]{0:T(1024)}, u32[]{:S(2)}) copy-start(f32[2048]{0:T(1024)} %param.22) | copy-start | bytes 24580
  107.5 11.9 all-to-all-start.2
  119.4 140.7 %all-to-all-start = ((bf16[3,8,128,512]{3,2,0,1:T(8,128)(2,1)}), bf16[3,8,128,512]{3,2,0,1:T(8,128)(2,1)S(1)}, u32[]{:S(2)}, u32[]{:S(2)}) async-start(bf16[3,8,128,512]{3,2,0,1:T(8,128)(2,1)} %select_bitcast_fusion), calls=%async_computation | async-start | bytes 6291456 | tf_op jit(solution)/shard_map/all_to_all | solution.py:138
  192.5 66.8 %copy-start.8 = (s32[2]{0:T(128)S(1)}, s32[2]{0:T(128)}, u32[]{:S(2)}) copy-start(s32[2]{0:T(128)} %copy-done.7) | copy-start | bytes 28
  260.0 135.7 %all-to-all-start.3 = ((bf16[8,2,512]{2,1,0:T(2,128)(2,1)}), bf16[8,2,512]{2,1,0:T(2,128)(2,1)}, u32[]{:S(2)}, u32[]{:S(2)}) async-start(bf16[8,2,512]{2,1,0:T(2,128)(2,1)} %reshape.531), calls=%async_computation.3 | async-start | bytes 32768 | tf_op jit(solution)/shard_map/all_to_all | solution.py:181
  275.0 9.9 copy-start
  298.4 14.3 %copy-start.3 = (bf16[1024,8,64]{0,2,1:T(8,128)(2,1)S(1)}, bf16[1024,8,64]{0,2,1:T(8,128)(2,1)}, u32[]{:S(2)}) copy-start(bf16[1024,8,64]{0,2,1:T(8,128)(2,1)} %reshape_squeeze.8) | copy-start | bytes 3145732
  335.6 3.9 copy-start.1
  343.4 1.3 copy-start.2
  351.4 3.9 copy-start.1
  359.2 1.3 copy-start.2
  367.1 3.9 copy-start.1
  375.0 1.3 copy-start.2
  382.9 3.9 copy-start.1
  390.8 1.3 copy-start.2
  392.1 7.9 copy-start.12
  395.7 19.6 %all-to-all-start.1 = ((bf16[8,128,512]{2,1,0:T(8,128)(2,1)}), bf16[8,128,512]{2,1,0:T(8,128)(2,1)S(1)}, u32[]{:S(2)}, u32[]{:S(2)}) async-start(bf16[8,128,512]{2,1,0:T(8,128)(2,1)} %copy.64), calls=%async_computation.1 | async-start | bytes 2097152 | tf_op jit(solution)/shard_map/all_to_all | solution.py:180
  399.9 311.8 %all-gather.19.cloned.1.call-start = ((), (), s32[]{:S(2)}) async-start(), calls=%async_computation.8 | async-start | bytes 21135360 | tf_op jit(solution)/shard_map/all_gather | solution.py:52
  422.2 383.5 %all-gather.15.cloned.1.call-start = ((), (), s32[]{:S(2)}) async-start(), calls=%async_computation.6 | async-start | bytes 18874368 | tf_op jit(solution)/shard_map/all_gather | solution.py:37
  422.8 439.1 %all-gather.17.cloned.1.call-start = ((), (), s32[]{:S(2)}) async-start(), calls=%async_computation.7 | async-start | bytes 9437184 | tf_op jit(solution)/shard_map/all_gather | solution.py:46
  423.3 301.0 %copy-start.5 = (bf16[2,2048]{1,0:T(2,128)(2,1)S(1)}, bf16[2,2048]{1,0:T(2,128)(2,1)}, u32[]{:S(2)}) copy-start(bf16[2,2048]{1,0:T(2,128)(2,1)} %param.21) | copy-start | bytes 24580
  423.4 746.9 %all-gather.21.cloned.1.call-start = ((), (), s32[]{:S(2)}) async-start(), calls=%async_computation.9 | async-start | bytes 21135360 | tf_op jit(solution)/shard_map/all_gather | solution.py:52
  724.3 81.4 %copy-start.11 = (f32[2048]{0:T(1024)S(1)}, f32[2048]{0:T(1024)}, u32[]{:S(2)}) copy-start(f32[2048]{0:T(1024)} %param.23) | copy-start | bytes 24580
Sparse Core Ops, SparseCore 0:
  9.9 49.3 all-gather.10
  61.2 27.9 all-gather.12
  422.3 289.3 all-gather.18
  713.5 92.1 all-gather.14
  807.4 54.3 all-gather.16
  879.7 290.4 all-gather.20
